TPU v7x, 256 devices: a whole 4x4x8 slice. The times are simulated.
256 devices in a mesh: dp: 16 (over z_lo, x), tensor: 16 (over y, z_hi, core).
Axes of the slice: x: 4, y: 4, z: 8 (z_hi: 2, z_lo: 4; z = z_hi * 4 + z_lo), core: 2. Of those that a mesh axis runs over, the one named last changes fastest.
Arguments:
- out_grad: bfloat16 [2048, 5120], P('dp'), may hold values from -6 to 6
- gate_act: bfloat16 [2048, 25600], P('dp', 'tensor'), may hold values from -6 to 6
- up_act: bfloat16 [2048, 25600], P('dp', 'tensor'), may hold values from -6 to 6
- codes: int32 [5120, 25600], P('dp', 'tensor'), may hold values from 0 to 15
- zero_points: int32 [5120, 400], P('dp', 'tensor'), may hold values from 0 to 15
- scales: float32 [5120, 400], P('dp', 'tensor'), may hold values from 0.0009782797 to 0.003913119
- rotation: bfloat16 [1600, 1600], replicated, may hold values from -0.15625 to 0.15625
Outputs:
- grad_gate: bfloat16 [2048, 25600], P('dp', 'tensor')
- grad_up: bfloat16 [2048, 25600], P('dp', 'tensor')
- log_scale_grad: float32 [5120, 400], P('dp', 'tensor')
All inputs are finite; a program needn't handle non-finite values.
Results may differ from a plain program's by a relative error of at most 0.011.
Values may be sent and summed in bfloat16 or wider, within the bound.
A program may use at most 128 MiB of HBM per device.

v0:
```python
import math

import jax
import jax.numpy as jnp
from jax import lax
from jax.sharding import PartitionSpec as P


def sylvester(order_size):
    indices = jnp.arange(order_size, dtype=jnp.int32)
    common_bits = indices[:, None] & indices[None, :]
    parity = jnp.zeros((order_size, order_size), jnp.int32)
    for bit_number in range(order_size.bit_length()):
        parity = parity + (common_bits >> bit_number & 1)
    return (1 - 2 * (parity % 2)).astype(jnp.float32)


def spread(blocks, block_size):
    tok_rows = blocks.shape[0]
    local_blocks = blocks.shape[1] // block_size
    devices = lax.axis_size("tensor")
    norm_factor = 1.0 / math.sqrt(devices * local_blocks)
    hadamard = sylvester(devices * local_blocks).reshape(
        devices, local_blocks, devices, local_blocks
    )
    stacked = blocks.reshape(1, tok_rows, local_blocks, block_size)
    summed = jnp.einsum(
        "qtjc,qjpk->ptkc",
        lax.all_to_all(stacked, "tensor", split_axis=3, concat_axis=0, tiled=True).astype(
            jnp.float32
        ),
        hadamard,
        precision=lax.Precision.HIGHEST,
    )
    summed = (summed * norm_factor).astype(jnp.bfloat16)
    result = lax.all_to_all(summed, "tensor", split_axis=0, concat_axis=3, tiled=True)
    return result.reshape(tok_rows, local_blocks * block_size)


def on_device(out_grad, gate_act, up_act, codes, zero_points, scales, rotation):
    columns = gate_act.shape[1]
    block_size = rotation.shape[0]
    feat_rows = codes.shape[0]
    groups_here = scales.shape[1]
    group_cols = columns // groups_here
    gate32 = gate_act.astype(jnp.float32)
    up32 = up_act.astype(jnp.float32)
    sigmoid_gate = jax.nn.sigmoid(gate32)
    hidden = (gate32 * sigmoid_gate * up32).astype(jnp.bfloat16)
    mixed = jnp.dot(hidden, rotation, preferred_element_type=jnp.float32)
    mixed = mixed.astype(jnp.bfloat16)
    rotated = spread(mixed, block_size)
    levels = (codes.reshape(feat_rows, groups_here, group_cols) - zero_points[:, :, None]).astype(
        jnp.float32
    )
    weight = (levels * scales[:, :, None]).astype(jnp.bfloat16).reshape(feat_rows, columns)
    grad_slice = lax.all_to_all(out_grad, "dp", split_axis=1, concat_axis=0, tiled=True)
    weight_grad = lax.dot_general(
        grad_slice,
        lax.all_gather(rotated, "dp", axis=0, tiled=True),
        (((0,), (0,)), ((), ())),
        preferred_element_type=jnp.float32,
    )
    log_scale_grad = (
        jnp.sum(weight_grad.reshape(feat_rows, groups_here, group_cols) * levels, axis=2) * scales
    )
    grad_rotated = lax.psum_scatter(
        jnp.dot(grad_slice, weight, preferred_element_type=jnp.float32),
        "dp",
        scatter_dimension=0,
        tiled=True,
    )
    grad_mixed = spread(grad_rotated.astype(jnp.bfloat16), block_size)
    grad_hidden = lax.dot_general(
        grad_mixed, rotation, (((1,), (1,)), ((), ())), preferred_element_type=jnp.float32
    )
    grad_gate = (grad_hidden * up32 * sigmoid_gate * (1.0 + gate32 * (1.0 - sigmoid_gate))).astype(
        jnp.bfloat16
    )
    grad_up = (grad_hidden * gate32 * sigmoid_gate).astype(jnp.bfloat16)
    return (grad_gate, grad_up, log_scale_grad)


def solution(mesh):
    return jax.shard_map(
        on_device,
        mesh=mesh,
        in_specs=(
            P("dp", None),
            P("dp", "tensor"),
            P("dp", "tensor"),
            P("dp", "tensor"),
            P("dp", "tensor"),
            P("dp", "tensor"),
            P(),
        ),
        out_specs=(P("dp", "tensor"), P("dp", "tensor"), P("dp", "tensor")),
        check_vma=False,
    )
```

profile of v0, /device:TPU:8, one launch (start us, length us, event | category | flops | bytes accessed | tf_op | source)
XLA Modules:
  0.0 394.8 jit_solution(10725968039748546528)
XLA Ops:
  7.2 2.4 copy.24
  9.6 8.5 %all-to-all-start = ((bf16[128,16,320]{0,2,1:T(8,128)(2,1)}), bf16[128,16,320]{0,2,1:T(8,128)(2,1)}, u32[]{:S(2)}, u32[]{:S(2)}) async-start(bf16[128,16,320]{0,2,1:T(8,128)(2,1)} %bitcast.4), calls=%async_computation | async-start | bytes 2621440 | tf_op jit(solution)/shard_map/all_to_all | solution.py:57
  18.2 2.4 copy.23
  20.6 1.3 fusion
  21.9 25.5 %all-to-all-done = bf16[128,16,320]{0,2,1:T(8,128)(2,1)} async-done(((bf16[128,16,320]{0,2,1:T(8,128)(2,1)}), bf16[128,16,320]{0,2,1:T(8,128)(2,1)}, u32[]{:S(2)}, u32[]{:S(2)}) %all-to-all-start) | async-done | bytes 1310752 | tf_op jit(solution)/shard_map/all_to_all | solution.py:57
  47.4 9.9 %convolution_bitcast_fusion = f32[2048,1600]{0,1:T(8,128)} fusion(bf16[320,1600]{0,1:T(8,128)(2,1)} %fusion, bf16[128,16,320]{0,2,1:T(8,128)(2,1)} %all-to-all-done), kind=kOutput, calls=%fused_computation | convolution fusion | flops 2097152000 | bytes 15441920 | tf_op jit(solution)/shard_map/dot_general | solution.py:68
  58.4 4.7 %fusion.2 = bf16[1,128,1,1600]{1,3,2,0:T(8,128)(2,1)S(1)} fusion(bf16[1600,1600]{1,0:T(8,128)(2,1)} %param.13, bf16[128,1600]{0,1:T(8,128)(2,1)S(1)} %copy-done.3, bf16[128,1600]{0,1:T(8,128)(2,1)S(1)} %copy-done.2), kind=kOutput, calls=%fused_computation.8 | convolution fusion | flops 657203200 | bytes 6348800 | tf_op jit(solution)/shard_map/dot_general | solution.py:50
  63.1 6.4 %copy.55 = bf16[1,128,1,1600]{1,2,0,3:T(2,128)(2,1)S(1)} copy(bf16[1,128,1,1600]{1,3,2,0:T(8,128)(2,1)S(1)} %fusion.2) | data formatting | bytes 819200 | tf_op jit(solution)/shard_map/reshape | solution.py:26
  70.0 9.9 %reduce.5 = bf16[1600,128]{1,0:T(8,128)(2,1)} reduce(bf16[1600,1,1,128]{3,2,1,0:T(2,128)(2,1)S(1)} %bitcast.84, bf16[]{:T(256)} %broadcast.409), dimensions={1,2}, to_apply=%bitcast.80.reduce_sub_computation | reduce | bytes 819202
  79.9 1.1 reshape.191
  81.0 24.9 %all_to_all.79 = bf16[16,2,6400]{2,1,0:T(2,128)(2,1)} all-to-all(bf16[16,2,6400]{2,1,0:T(2,128)(2,1)S(1)} %reshape.191), channel_id=1, replica_groups=mesh['dp'=16,'tensor'=16] {'tensor'}, dimensions={0} | all-to-all | bytes 819200 | tf_op jit(solution)/shard_map/all_to_all | solution.py:29
  105.9 2.7 reshape.192
  108.6 7.6 %bitcast_reduce_fusion = bf16[128,1600]{0,1:T(8,128)(2,1)} fusion(bf16[1600,1,1,128]{3,2,1,0:T(2,128)(2,1)S(1)} %reshape.192), kind=kLoop, calls=%fused_computation.60 | loop fusion | bytes 819200 | tf_op jit(solution)/shard_map/all_to_all | solution.py:29
  116.2 1.1 all_to_all.69
  117.9 21.3 %all_to_all.80 = bf16[16,128,1,100]{1,3,2,0:T(8,128)(2,1)S(1)} all-to-all(bf16[16,128,1,100]{1,3,2,0:T(8,128)(2,1)S(1)} %copy.31), channel_id=1, replica_groups=mesh['dp'=16,'tensor'=16] {'tensor'}, dimensions={0} | all-to-all | bytes 819200 | tf_op jit(solution)/shard_map/all_to_all | solution.py:36
  139.2 0.8 reshape.183
  140.1 79.6 %reduce-scatter.2.cloned.1.call-done = f32[128,1600]{0,1:T(8,128)} async-done(((f32[2048,1600]{0,1:T(8,128)}), f32[128,1600]{0,1:T(8,128)}) %reduce-scatter.2.cloned.1.call-update) | async-done | bytes 819216 | tf_op jit(solution)/shard_map/reduce_scatter | solution.py:67
  219.7 1.2 convert_bitcast_fusion
  220.9 6.4 %copy.56 = bf16[1,128,1,1600]{1,2,0,3:T(2,128)(2,1)S(1)} copy(bf16[1,128,1,1600]{1,3,2,0:T(8,128)(2,1)S(1)} %convert_bitcast_fusion) | data formatting | bytes 819200 | tf_op jit(solution)/shard_map/reshape | solution.py:26
  227.3 9.9 %reduce.4 = bf16[1600,128]{1,0:T(8,128)(2,1)} reduce(bf16[1600,1,1,128]{3,2,1,0:T(2,128)(2,1)S(1)} %bitcast.85, bf16[]{:T(256)} %broadcast.409), dimensions={1,2}, to_apply=%bitcast.81.reduce_sub_computation | reduce | bytes 819202
  237.2 1.1 reshape.189
  238.3 18.4 %all_to_all.81 = bf16[16,2,6400]{2,1,0:T(2,128)(2,1)} all-to-all(bf16[16,2,6400]{2,1,0:T(2,128)(2,1)S(1)} %reshape.189), channel_id=1, replica_groups=mesh['dp'=16,'tensor'=16] {'tensor'}, dimensions={0} | all-to-all | bytes 819200 | tf_op jit(solution)/shard_map/all_to_all | solution.py:29
  256.7 2.7 reshape.190
  259.4 7.6 %bitcast_reduce_fusion.1 = bf16[128,1600]{0,1:T(8,128)(2,1)} fusion(bf16[1600,1,1,128]{3,2,1,0:T(2,128)(2,1)S(1)} %reshape.190), kind=kLoop, calls=%fused_computation.61 | loop fusion | bytes 819200 | tf_op jit(solution)/shard_map/all_to_all | solution.py:29
  267.0 1.1 all_to_all.63
  268.6 0.9 copy.28
  269.4 7.6 %all-to-all-start.2 = ((bf16[16,128,1,100]{1,3,2,0:T(8,128)(2,1)}), bf16[16,128,1,100]{1,3,2,0:T(8,128)(2,1)S(1)}, u32[]{:S(2)}, u32[]{:S(2)}) async-start(bf16[16,128,1,100]{1,3,2,0:T(8,128)(2,1)} %copy.28), calls=%async_computation.3 | async-start | bytes 851968 | tf_op jit(solution)/shard_map/all_to_all | solution.py:36
  277.0 91.9 %all-gather.2.cloned.1.call-done = bf16[2048,1600]{0,1:T(8,128)(2,1)} async-done(((bf16[128,1600]{0,1:T(8,128)(2,1)}), bf16[2048,1600]{0,1:T(8,128)(2,1)}) %all-gather.2.cloned.1.call-update) | async-done | bytes 6553616 | tf_op jit(solution)/shard_map/all_gather | solution.py:60
  368.9 7.1 %convolution_bitcast_fusion.1 = f32[320,1600]{1,0:T(8,128)} fusion(bf16[2048,1600]{0,1:T(8,128)(2,1)} %all-gather.2.cloned.1.call-done, bf16[128,16,320]{0,2,1:T(8,128)(2,1)} %all-to-all-done), kind=kOutput, calls=%fused_computation.1 | convolution fusion | flops 2097152000 | bytes 9912320 | tf_op jit(solution)/shard_map/dot_general | solution.py:58
  376.0 3.1 copy.32
  379.1 2.3 multiply_reduce_fusion
  382.2 5.3 %fusion.20 = (bf16[128,1600]{0,1:T(8,128)(2,1)}, bf16[128,1600]{0,1:T(8,128)(2,1)}) fusion(bf16[128,1600]{0,1:T(8,128)(2,1)} %param.8, bf16[128,1600]{0,1:T(8,128)(2,1)} %param.9, bf16[1600,1600]{1,0:T(8,128)(2,1)} %param.13, bf16[128,1600]{0,1:T(8,128)(2,1)S(1)} %reshape.180), kind=kOutput, calls=%fused_computation.34 | convolution fusion | flops 658432000 | bytes 7168000 | tf_op jit(solution)/shard_map/dot_general | solution.py:74
  (19 shorter events, 3.5 us)
Async XLA Ops:
  9.6 37.8 %all-to-all-start = ((bf16[128,16,320]{0,2,1:T(8,128)(2,1)}), bf16[128,16,320]{0,2,1:T(8,128)(2,1)}, u32[]{:S(2)}, u32[]{:S(2)}) async-start(bf16[128,16,320]{0,2,1:T(8,128)(2,1)} %bitcast.4), calls=%async_computation | async-start | bytes 2621440 | tf_op jit(solution)/shard_map/all_to_all | solution.py:57
  18.1 2.4 copy-start
  18.1 2.4 copy-start.1
  18.1 201.5 %reduce-scatter.2.cloned.1.call-start = ((), (), s32[]{:S(2)}) async-start(), calls=%async_computation.6 | async-start | bytes 13926400 | tf_op jit(solution)/shard_map/reduce_scatter | solution.py:67
  57.3 1.0 copy-start.2
  57.3 1.1 copy-start.3
  57.3 311.6 %all-gather.2.cloned.1.call-start = ((), (), s32[]{:S(2)}) async-start(), calls=%async_computation.7 | async-start | bytes 6963200 | tf_op jit(solution)/shard_map/all_gather | solution.py:60
  269.4 112.7 %all-to-all-start.2 = ((bf16[16,128,1,100]{1,3,2,0:T(8,128)(2,1)}), bf16[16,128,1,100]{1,3,2,0:T(8,128)(2,1)S(1)}, u32[]{:S(2)}, u32[]{:S(2)}) async-start(bf16[16,128,1,100]{1,3,2,0:T(8,128)(2,1)} %copy.28), calls=%async_computation.3 | async-start | bytes 851968 | tf_op jit(solution)/shard_map/all_to_all | solution.py:36
Sparse Core Ops, SparseCore 0:
  57.4 162.2 reduce-scatter.1
  222.0 146.9 all-gather.1
where the time goes:
time: 401 us; the launch traced here: 395 us
  waiting for transfers between devices  197 us (49%)
  blocking collectives  64.5 us (16%)
  local copies, waits for them, and re-layouts  49 us (12%)
  matrix products  28 us (7%)
  other arithmetic  25.3 us (6%)
  starting transfers between devices  16.4 us (4%)
  between operations  14.6 us (4%)
    all_gather x1, waiting for transfers between devices, on_device(): lax.all_gather(rotated, 'dp', axis=0, tiled=True)  91.9 us
    reduce_scatter x1, waiting for transfers between devices, on_device(): lax.psum_scatter(jnp.dot(grad_slice, weight, preferred_element_type=jnp.f...  79.6 us
    all_to_all x2, blocking collectives, spread(): lax.all_to_all(stacked, 'tensor', split_axis=3, concat_axis=0, tiled=True)  43.2 us
    all_to_all x1, waiting for transfers between devices, on_device(): lax.all_to_all(out_grad, 'dp', split_axis=1, concat_axis=0, tiled=True)  25.5 us
    all_to_all x1, blocking collectives, spread(): lax.all_to_all(summed, 'tensor', split_axis=0, concat_axis=3, tiled=True)  21.3 us
    unnamed x2, other arithmetic  19.8 us
    all_to_all x4, local copies, waits for them, and re-layouts, spread(): lax.all_to_all(stacked, 'tensor', split_axis=3, concat_axis=0, tiled=True)  17.3 us
    unnamed x15, local copies, waits for them, and re-layouts  13.9 us
  transfers between devices with their start and end apart: 4, of which 3 were waited for; matrix products, arithmetic and copies ran while one was open for 21% of the time, Pallas kernels for 0%

commit v1 on v0

v1 whole, which is shorter than its diff:
```python
import functools

import jax
import jax.numpy as jnp
from jax import lax
from jax.experimental import pallas as pl
from jax.experimental.pallas import tpu as pltpu
from jax.sharding import PartitionSpec as P

MESH = pl.DeviceIdType.MESH
F32 = jnp.float32
BF16 = jnp.bfloat16
TOK = 128
BLK = 1600
QR = 400
LO = 208
DROW = 320
DG = 1280
NC = 4
CR = BLK // NC
N_COPY = 110


def kernel(
    og_in, g_in, u_in, wmain, wrem, rot,
    o_gg, o_gu, o_ls,
    wfull, wrecv, og, m_buf, c_buf, yv, yo, h_buf, fp, fm, rott, pk,
    sp, sm, rp, rm, g_buf, a1, a2, s3, lsb, ssem, rsem,
):
    dp = lax.axis_index("dp")
    tn = lax.axis_index("tensor")
    x, zl = lax.rem(dp, 4), lax.div(dp, 4)
    y, zh, c = lax.div(tn, 4), lax.rem(lax.div(tn, 2), 2), lax.rem(tn, 2)
    pos = zh * 4 + zl

    def at_x(k):
        return (zl * 4 + lax.rem(x + 4 + k, 4), tn)

    def at_y(k):
        return (dp, lax.rem(y + 4 + k, 4) * 4 + zh * 2 + c)

    def at_z(k):
        to = lax.rem(pos + 8 + k, 8)
        return (lax.rem(to, 4) * 4 + x, y * 4 + lax.div(to, 4) * 2 + c)

    other = (dp, y * 4 + zh * 2 + 1 - c)

    count = [0]
    pending = []

    def send(src, dst, device):
        i = count[0]
        count[0] += 1
        copy = pltpu.make_async_remote_copy(
            src_ref=src, dst_ref=dst, send_sem=ssem.at[i], recv_sem=rsem.at[i],
            device_id=device, device_id_type=MESH,
        )
        copy.start()
        pending.append(copy)
        return copy

    barrier = pltpu.get_barrier_semaphore()
    peers = [at_x(1), at_x(2), at_x(3), at_y(1), at_y(2), at_y(3)]
    peers += [at_z(1), at_z(-1), at_z(2), at_z(-2), other]
    for peer in peers:
        pl.semaphore_signal(barrier, inc=1, device_id=peer, device_id_type=MESH)
    pl.semaphore_wait(barrier, len(peers))

    tile = lax.div(x, 2) * 5 + lax.rem(x, 2) * 3

    def main_at(j, q):
        xs = lax.rem(x + 4 + j, 4)
        at = pl.multiple_of((lax.div(xs, 2) * 5 + lax.rem(xs, 2) * 3) * 128, 128)
        return wfull.at[pl.ds(q * QR, QR), pl.ds(at, 256)]

    def rem_at(j, q):
        return wrecv.at[lax.rem(x + 4 + j, 4), q]

    w_plus, w_minus = [], []
    for q in range(4):
        own = wmain.at[pl.ds(q * QR, QR)]
        w_plus.append((send(own, main_at(0, q), at_x(1)), send(wrem.at[q], rem_at(0, q), at_x(1))))
        w_minus.append((send(own, main_at(0, q), at_x(-1)), send(wrem.at[q], rem_at(0, q), at_x(-1))))

    def og_cols(k):
        return pl.ds(pl.multiple_of(lax.rem(zl + 4 + k, 4) * DG, 128), DG)

    og_copies = [
        send(og_in.at[:, og_cols(1)], og.at[3], at_z(1)),
        send(og_in.at[:, og_cols(-1)], og.at[1], at_z(-1)),
        send(og_in.at[pl.ds(0, 64), og_cols(2)], og.at[2, pl.ds(0, 64)], at_z(2)),
        send(og_in.at[pl.ds(64, 64), og_cols(2)], og.at[2, pl.ds(64, 64)], at_z(-2)),
    ]

    def hidden_rows(i, _):
        rows = pl.ds(pl.multiple_of(i * 320, 16), 320)
        gate = g_in[rows, :].astype(F32)
        up = u_in[rows, :].astype(F32)
        sig = 1.0 / (1.0 + jnp.exp(-gate))
        gs = gate * sig
        m_buf[rows, :] = (gs * up).astype(BF16)
        a1[rows, :] = up * sig * (1.0 + gate * (1.0 - sig))
        a2[rows, :] = gs
        return 0

    lax.fori_loop(0, 5, hidden_rows, 0)
    hid = m_buf[...].astype(F32).T.astype(BF16)

    def mixed_cols(i, _):
        cols = pl.ds(pl.multiple_of(i * 256, 256), 256)
        part = jnp.dot(hid, rot[:, cols], preferred_element_type=F32)
        m_buf[pl.ds(pl.multiple_of(i * 256, 256), 256), :] = part.T.astype(BF16)
        return 0

    lax.fori_loop(0, 6, mixed_cols, 0)
    part = jnp.dot(hid, rot[:, 1536:1600], preferred_element_type=F32)
    m_buf[1536:1600, :] = part.T.astype(BF16)

    at_own = pl.multiple_of(tile * 128, 128)
    wfull[:, pl.ds(at_own, 256)] = wmain[...]
    wrecv[x] = wrem[...]
    og[0] = og_in[:, og_cols(0)]

    sign_c = jnp.where(c == 1, -1.0, 1.0).astype(F32)

    def over_core_and_y(src, slot, scale, dst):
        exchange = send(src, c_buf.at[slot], other)
        exchange.wait_recv()
        vals = yv.at[slot]
        outs = yo.at[slot]
        for q in range(4):
            rows = pl.ds(q * QR, QR)
            mine = src[rows, :].astype(F32) * sign_c + c_buf[slot, rows, :].astype(F32)
            outs[0, q] = mine.astype(BF16)
        copies = [
            send(outs.at[0, lax.rem(y + k, 4)], vals.at[y], at_y(k)) for k in (1, 3, 2)
        ]
        vals[y] = outs[0, y]
        for copy in copies:
            copy.wait_recv()
        v = [vals[i].astype(F32) for i in range(4)]
        p0, p1, n0, n1 = v[0] + v[1], v[2] + v[3], v[0] - v[1], v[2] - v[3]
        for i, value in enumerate((p0 + p1, n0 + n1, p0 - p1, n0 - n1)):
            outs[1, i] = (value * scale).astype(BF16)
        mine_at = pl.ds(pl.multiple_of(y * QR, 16), QR)
        copies = [
            send(outs.at[1, lax.rem(y + k, 4)], dst.at[mine_at], at_y(k)) for k in (1, 3, 2)
        ]
        dst[mine_at, :] = outs[1, y]
        return copies

    back = over_core_and_y(m_buf, 0, 1.0, h_buf)
    for copy in back:
        copy.wait_recv()

    def rows_of(n):
        return pl.ds(n * CR, CR)

    half_a, half_b = range(NC // 2), range(NC // 2, NC)
    got_p, got_m = {}, {}
    for n in range(NC):
        got_p[1, n] = send(h_buf.at[rows_of(n)], fp.at[0, rows_of(n)], at_z(1))
        got_m[1, n] = send(h_buf.at[rows_of(n)], fm.at[0, rows_of(n)], at_z(-1))

    w_two = []
    for q in (0, 1):
        for copy in w_plus[q]:
            copy.wait_recv()
        w_two.append((send(main_at(-1, q), main_at(-1, q), at_x(1)), send(rem_at(-1, q), rem_at(-1, q), at_x(1))))
    for q in (2, 3):
        for copy in w_minus[q]:
            copy.wait_recv()
        w_two.append((send(main_at(1, q), main_at(1, q), at_x(-1)), send(rem_at(1, q), rem_at(1, q), at_x(-1))))

    for k in (1, 2, 3):
        for n in range(NC):
            got_p[k, n].wait_recv()
            if k < 3 or n in half_a:
                got_p[k + 1, n] = send(fp.at[k - 1, rows_of(n)], fp.at[k, rows_of(n)], at_z(1))
            got_m[k, n].wait_recv()
            if k < 3 or n in half_b:
                got_m[k + 1, n] = send(fm.at[k - 1, rows_of(n)], fm.at[k, rows_of(n)], at_z(-1))

    for q in (2, 3):
        for copy in w_plus[q]:
            copy.wait_recv()
    for q in (0, 1):
        for copy in w_minus[q]:
            copy.wait_recv()
    for copies in w_two:
        for copy in copies:
            copy.wait_recv()
    for copy in og_copies:
        copy.wait_recv()
    low = lax.broadcasted_iota(jnp.int32, (LO, 128), 1) < 64
    for q in range(4):
        for pair in range(2):
            first = wrecv[2 * pair, q].astype(F32)
            second = wrecv[2 * pair + 1, q].astype(F32)
            lanes = pl.ds((pair * 5 + 2) * 128, 128)
            wfull[pl.ds(q * QR, LO), lanes] = jnp.where(low, first, second).astype(BF16)
            turned = pltpu.roll(jnp.where(low, second, first), 64, 1)
            wfull[pl.ds(q * QR + LO, QR - LO), lanes] = turned[: QR - LO].astype(BF16)
    og_all = og.reshape(4 * TOK, DG)
    for q in range(4):
        rows = pl.ds(q * QR, QR)
        part = lax.dot_general(
            wfull[rows, :], og_all[...], (((1,), (1,)), ((), ())), preferred_element_type=F32
        )
        for k in range(4):
            pk[k, rows, :] = part[:, k * TOK : (k + 1) * TOK]

    def sign_of(at):
        far = lax.div(lax.rem(pos + 8 + at, 8), 4)
        return jnp.where(far * zh == 1, -1.0, 1.0).astype(F32)

    sum_p, sum_m = {}, {}

    def send_p(d, n, add):
        value = pk[d % 4, rows_of(n), :] * sign_of(d)
        if add:
            sum_p[d, n].wait_recv()
            value = value + rp[d, rows_of(n), :].astype(F32)
        sp[d - 1, rows_of(n), :] = value.astype(BF16)
        sum_p[d - 1, n] = send(sp.at[d - 1, rows_of(n)], rp.at[d - 1, rows_of(n)], at_z(1))

    def send_m(d, n, add):
        value = pk[-d % 4, rows_of(n), :] * sign_of(-d)
        if add:
            sum_m[d, n].wait_recv()
            value = value + rm[d, rows_of(n), :].astype(F32)
        sm[d - 1, rows_of(n), :] = value.astype(BF16)
        sum_m[d - 1, n] = send(sm.at[d - 1, rows_of(n)], rm.at[d - 1, rows_of(n)], at_z(-1))

    for na, nb in zip(half_a, half_b):
        send_p(4, na, False)
        send_m(4, nb, False)
    for na, nb in zip(half_a, half_b):
        send_p(3, nb, False)
        send_m(3, na, False)

    for n in half_a:
        got_p[4, n].wait_recv()
    for n in half_b:
        got_m[4, n].wait_recv()

    def rotated(k):
        mine = h_buf if k == 0 else fm.at[k - 1]
        su, sv = sign_of(k) * 0.25, sign_of(k + 4) * 0.25
        lanes = pl.ds(k * TOK, TOK)
        for n in range(NC):
            if k == 0:
                far = fp if n in half_a else fm
                other_side = far[3, rows_of(n), :]
            else:
                other_side = fp[3 - k, rows_of(n), :]
            value = mine[rows_of(n), :].astype(F32) * su + other_side.astype(F32) * sv
            rott[rows_of(n), lanes] = value.astype(BF16)

    def weight_grad(i, _):
        rows = pl.ds(pl.multiple_of(i * 320, 16), 320)
        part = jnp.dot(rott[rows, :], og_all[...], preferred_element_type=F32)
        part = part * wfull[rows, :].astype(F32)
        s3[i, 0:5, :] = jnp.sum(part.reshape(5, 64, DG), axis=1)
        return 0

    for na, nb in zip(half_a, half_b):
        send_p(3, na, True)
        send_m(3, nb, True)
    for k in range(4):
        rotated(k)
    for na, nb in zip(half_a, half_b):
        send_p(2, nb, True)
        send_m(2, na, True)
    s3[...] = jnp.zeros_like(s3)
    lax.fori_loop(0, 3, weight_grad, 0)
    for na, nb in zip(half_a, half_b):
        send_p(2, na, True)
        send_m(2, nb, True)
    lax.fori_loop(3, 5, weight_grad, 0)

    def s_lanes(j):
        xs = lax.rem(x + 4 + j, 4)
        return pl.ds(pl.multiple_of((lax.div(xs, 2) * 5 + lax.rem(xs, 2) * 2) * 128, 128), 384)

    ls_copies = [
        send(s3.at[:, :, s_lanes(j)], lsb.at[j - 1], at_x(j)) for j in (1, 2, 3)
    ]
    for na, nb in zip(half_a, half_b):
        send_p(1, nb, True)
        send_m(1, na, True)
    for na, nb in zip(half_a, half_b):
        send_p(1, na, True)
        send_m(1, nb, True)
    for n in range(NC):
        sum_p[0, n].wait_recv()
        sum_m[0, n].wait_recv()
        value = pk[0, rows_of(n), :] * sign_of(0)
        value = value + rp[0, rows_of(n), :].astype(F32) + rm[0, rows_of(n), :].astype(F32)
        g_buf[0, rows_of(n), :] = value.astype(BF16)

    back = over_core_and_y(g_buf.at[0], 1, 0.25, g_buf.at[1])
    for copy in ls_copies:
        copy.wait_recv()
    total = s3[:, :, s_lanes(0)]
    for j in range(3):
        total = total + lsb[j]
    total = total.reshape(40, 384)
    turned = pltpu.roll(total, 320, 1)
    total = jnp.where(lax.rem(x, 2) == 1, turned, total)[:, :DROW]
    for i in range(5):
        rows = slice(5 * i, 5 * i + 5)
        o_ls[rows, :] = total[8 * i : 8 * i + 5, :]
    for copy in back:
        copy.wait_recv()

    def last_rows(i, _):
        rows = pl.ds(pl.multiple_of(i * 320, 16), 320)
        grad = jnp.dot(rot[rows, :], g_buf[1], preferred_element_type=F32)
        o_gg[rows, :] = (grad * a1[rows, :]).astype(BF16)
        o_gu[rows, :] = (grad * a2[rows, :]).astype(BF16)
        return 0

    lax.fori_loop(0, 5, last_rows, 0)
    for copy in pending:
        copy.wait_send()


def on_device(out_grad, gate_act, up_act, codes, zero_points, scales, rotation):
    levels = (codes.reshape(DROW, 25, 64) - zero_points[:, :, None]).astype(F32)
    weight = (levels * scales[:, :, None]).astype(BF16).reshape(DROW, BLK).T
    odd = lax.axis_index("dp") % 2 == 1
    wmain = jnp.where(odd, weight[:, 64:], weight[:, :256])
    rest = jnp.where(odd, weight[:, :64], weight[:, 256:]).reshape(4, QR, 64)
    first = rest[:, :LO]
    second = jnp.pad(rest[:, LO:], ((0, 0), (0, 2 * LO - QR), (0, 0)))
    wrem = jnp.where(
        odd, jnp.concatenate([second, first], 2), jnp.concatenate([first, second], 2)
    )
    vm = pl.BlockSpec(memory_space=pltpu.VMEM)
    gg, gu, ls = pl.pallas_call(
        kernel,
        out_shape=(
            jax.ShapeDtypeStruct((BLK, TOK), BF16),
            jax.ShapeDtypeStruct((BLK, TOK), BF16),
            jax.ShapeDtypeStruct((25, DROW), F32),
        ),
        in_specs=[vm] * 6,
        out_specs=(vm, vm, vm),
        scratch_shapes=[
            pltpu.VMEM((BLK, DG), BF16),
            pltpu.VMEM((4, 4, LO, 128), BF16),
            pltpu.VMEM((4, TOK, DG), BF16),
            pltpu.VMEM((BLK, TOK), BF16),
            pltpu.VMEM((2, BLK, TOK), BF16),
            pltpu.VMEM((2, 4, QR, TOK), BF16),
            pltpu.VMEM((2, 2, 4, QR, TOK), BF16),
            pltpu.VMEM((BLK, TOK), BF16),
            pltpu.VMEM((4, BLK, TOK), BF16),
            pltpu.VMEM((4, BLK, TOK), BF16),
            pltpu.VMEM((BLK, 4 * TOK), BF16),
            pltpu.VMEM((4, BLK, TOK), F32),
            pltpu.VMEM((4, BLK, TOK), BF16),
            pltpu.VMEM((4, BLK, TOK), BF16),
            pltpu.VMEM((4, BLK, TOK), BF16),
            pltpu.VMEM((4, BLK, TOK), BF16),
            pltpu.VMEM((2, BLK, TOK), BF16),
            pltpu.VMEM((BLK, TOK), F32),
            pltpu.VMEM((BLK, TOK), F32),
            pltpu.VMEM((5, 8, DG), F32),
            pltpu.VMEM((3, 5, 8, 384), F32),
            pltpu.SemaphoreType.DMA((N_COPY,)),
            pltpu.SemaphoreType.DMA((N_COPY,)),
        ],
        name="whole",
        compiler_params=pltpu.CompilerParams(
            collective_id=0, has_side_effects=True, vmem_limit_bytes=56 << 20
        ),
    )(out_grad, gate_act.T, up_act.T, wmain, wrem, rotation)
    return gg.T, gu.T, ls.T


def solution(mesh):
    return jax.shard_map(
        on_device,
        mesh=mesh,
        in_specs=(
            P("dp", None),
            P("dp", "tensor"),
            P("dp", "tensor"),
            P("dp", "tensor"),
            P("dp", "tensor"),
            P("dp", "tensor"),
            P(),
        ),
        out_specs=(P("dp", "tensor"), P("dp", "tensor"), P("dp", "tensor")),
        check_vma=False,
    )
```

time: 401 us -> 129 us (0.32)
  waiting for transfers between devices: 197 us -> 0 us
  Pallas kernels: 0 us -> 113 us
  blocking collectives: 64.5 us -> 0 us
  local copies, waits for them, and re-layouts: 49 us -> 8.23 us
  matrix products: 28 us -> 0 us
  other arithmetic: 25.3 us -> 4.16 us
  starting transfers between devices: 16.4 us -> 0 us
  between operations: 14.6 us -> 0.7 us
    pallas_call x0 -> x1, Pallas kernels: none -> 113 us  [on_device(): pl.pallas_call(kernel, out_shape=(jax.ShapeDtypeStruct((BLK, TOK), BF16),...]
    all_gather x1 -> x0, waiting for transfers between devices: 91.9 us -> none  [on_device(): lax.all_gather(rotated, 'dp', axis=0, tiled=True)]
    reduce_scatter x1 -> x0, waiting for transfers between devices: 79.6 us -> none  [on_device(): lax.psum_scatter(jnp.dot(grad_slice, weight, preferred_element_type=jnp.f...]
    all_to_all x3 -> x0, blocking collectives: 64.5 us -> none  [the longest x2 43.2 us: spread(): lax.all_to_all(stacked, 'tensor', split_axis=3, concat_axis=0, tiled=True)]
    dot_general x6 -> x0, matrix products: 28 us -> none  [the longest x1 9.91 us: on_device(): jnp.dot(grad_slice, weight, preferred_element_type=jnp.float32)]
    all_to_all x2 -> x0, waiting for transfers between devices: 25.5 us -> none  [the longest x1 25.5 us: on_device(): lax.all_to_all(out_grad, 'dp', split_axis=1, concat_axis=0, tiled=True)]
    unnamed x2 -> x0, other arithmetic: 19.8 us -> none
    all_to_all x4 -> x0, local copies, waits for them, and re-layouts: 17.3 us -> none  [spread(): lax.all_to_all(stacked, 'tensor', split_axis=3, concat_axis=0, tiled=True)]
  transfers between devices with their start and end apart: 4 -> 0, of which waited for: 3 -> 0; matrix products, arithmetic and copies ran while one was open for 21% -> 0% of each run, Pallas kernels for 0% -> 0%
where the time goes in v1:
time: 129 us; the launch traced here: 127 us
  Pallas kernels  113 us (88%)
  local copies, waits for them, and re-layouts  8.23 us (6%)
  other arithmetic  4.16 us (3%)
    pallas_call x1, Pallas kernels, on_device(): pl.pallas_call(kernel, out_shape=(jax.ShapeDtypeStruct((BLK, TOK), BF16),...  113 us
    unnamed x8, local copies, waits for them, and re-layouts  8.16 us

profile of v1, /device:TPU:8, one launch (start us, length us, event | category | flops | bytes accessed | tf_op | source)
XLA Modules:
  0.0 126.5 jit_solution(8379041142201363328)
XLA Ops:
  0.6 0.0 copy-start
  0.6 0.0 copy-start.1
  0.7 3.2 %copy.10 = s32[320,1600]{0,1:T(8,128)} copy(s32[320,1600]{1,0:T(8,128)} %param.10) | data formatting | bytes 4096000 | tf_op args[3]
  3.8 0.0 copy-done
  3.8 0.0 copy-done.1
  3.8 2.0 %fusion = bf16[320,1600]{0,1:T(8,128)(2,1)S(1)} fusion(s32[320,1600]{0,1:T(8,128)} %copy.10, f32[320,25]{0,1:T(8,128)S(1)} %copy-done, s32[320,25]{0,1:T(8,128)S(1)} %copy-done.1), kind=kLoop, calls=%fused_computation.1 | loop fusion | flops 2048000 | bytes 3136000 | tf_op jit(solution)/shard_map/convert_element_type | solution.py:331
  5.8 1.2 slice_select_fusion.wmain
  7.0 0.1 slice_select_fusion.1
  7.2 0.9 maximum_select_fusion.wrem
  8.1 113.4 %whole.1 = (bf16[1600,128]{1,0:T(8,128)(2,1)}, bf16[1600,128]{1,0:T(8,128)(2,1)}, f32[25,320]{1,0:T(8,128)}) custom-call(bf16[128,5120]{1,0:T(8,128)(2,1)} %og_in.1, bf16[1600,128]{1,0:T(8,128)(2,1)} %bitcast.23, bf16[1600,128]{1,0:T(8,128)(2,1)} %bitcast.24, bf16[1600,256]{1,0:T(8,128)(2,1)} %slice_select_fusion.wmain, ...), custom_call_target="tpu_custom_call" | custom-call | tf_op jit(solution)/shard_map/whole/pallas_call | solution.py:341
  121.5 1.8 %copy.14 = bf16[128,1600]{0,1:T(8,128)(2,1)} copy(bf16[128,1600]{0,1:T(8,128)(2,1)} %bitcast.22) | data formatting | bytes 819200
  123.3 1.8 %copy.15 = bf16[128,1600]{0,1:T(8,128)(2,1)} copy(bf16[128,1600]{0,1:T(8,128)(2,1)} %bitcast.21) | data formatting | bytes 819200
  125.1 1.4 %copy.16 = f32[320,25]{0,1:T(8,128)} copy(f32[320,25]{0,1:T(8,128)} %bitcast.25) | data formatting | bytes 64000
  (3 shorter events, 0.1 us)
Async XLA Ops:
  0.6 3.2 %copy-start = (f32[320,25]{0,1:T(8,128)S(1)}, f32[320,25]{0,1:T(8,128)}, u32[]{:S(2)}) copy-start(f32[320,25]{0,1:T(8,128)} %param.12) | copy-start | bytes 96004
  0.6 3.2 %copy-start.1 = (s32[320,25]{0,1:T(8,128)S(1)}, s32[320,25]{0,1:T(8,128)}, u32[]{:S(2)}) copy-start(s32[320,25]{0,1:T(8,128)} %param.11) | copy-start | bytes 96004

commit v2 on v0

v2 whole, which is shorter than its diff:
```python
import jax
import jax.numpy as jnp
from jax import lax
from jax.experimental import pallas as pl
from jax.experimental.pallas import tpu as pltpu
from jax.sharding import PartitionSpec as P

MESH = pl.DeviceIdType.MESH
F32 = jnp.float32
BF16 = jnp.bfloat16
TOK = 128
BLK = 1600
DROW = 320
DG = 1280
REST = 832
HALF_A, HALF_B = (0, 2), (1, 3)
N_COPY = 154


def rows_of(n):
    return pl.ds(384 * n, size_of(n))


def size_of(n):
    return 384 if n < 3 else 448


def kernel(
    og_in, g_in, u_in, codes_in, zp_in, sc_in, rot_in,
    o_gg, o_gu, o_ls,
    codes, rot, g_v, u_v, wfull, wrecv, og, hid, m_buf, c_buf, mix, yv, yo, h_buf, fp, fm, rott, pk,
    sp, sm, rp, rm, g_buf, a1, a2, s3, lsb, zps, scs, lsem, ssem, rsem,
):
    dp = lax.axis_index("dp")
    tn = lax.axis_index("tensor")
    x, zl = lax.rem(dp, 4), lax.div(dp, 4)
    y, zh, c = lax.div(tn, 4), lax.rem(lax.div(tn, 2), 2), lax.rem(tn, 2)
    pos = zh * 4 + zl
    odd = lax.rem(x, 2)

    def at_x(k):
        return (zl * 4 + lax.rem(x + 4 + k, 4), tn)

    def at_y(k):
        return (dp, lax.rem(y + 4 + k, 4) * 4 + zh * 2 + c)

    def at_z(k):
        to = lax.rem(pos + 8 + k, 8)
        return (lax.rem(to, 4) * 4 + x, y * 4 + lax.div(to, 4) * 2 + c)

    other = (dp, y * 4 + zh * 2 + 1 - c)

    def og_cols(k):
        return pl.ds(pl.multiple_of(lax.rem(zl + 4 + k, 4) * DG, 128), DG)

    loads = [
        pltpu.make_async_copy(src, dst, lsem.at[i])
        for i, (src, dst) in enumerate(
            ((codes_in, codes), (g_in, g_v), (u_in, u_v), (rot_in, rot), (og_in.at[:, og_cols(0)], og.at[0]))
        )
    ]
    for load in loads:
        load.start()

    count = [0]
    pending = []

    def send(src, dst, device):
        i = count[0]
        count[0] += 1
        copy = pltpu.make_async_remote_copy(
            src_ref=src, dst_ref=dst, send_sem=ssem.at[i], recv_sem=rsem.at[i],
            device_id=device, device_id_type=MESH,
        )
        copy.start()
        pending.append(copy)
        return copy

    barrier = pltpu.get_barrier_semaphore()
    peers = [at_x(1), at_x(2), at_x(3), at_y(1), at_y(2), at_y(3)]
    peers += [at_z(1), at_z(-1), at_z(2), at_z(-2), other]
    for peer in peers:
        pl.semaphore_signal(barrier, inc=1, device_id=peer, device_id_type=MESH)
    pl.semaphore_wait(barrier, len(peers))

    half = pl.ds(pl.multiple_of(c * 64, 64), 64)
    first, second = (pl.ds(pl.multiple_of(c * 64 + i * 32, 32), 32) for i in (0, 1))
    og_far = [
        (send(og_in.at[half, og_cols(1)], og.at[3, half], at_z(1)),),
        (send(og_in.at[half, og_cols(-1)], og.at[1, half], at_z(-1)),),
        (
            send(og_in.at[first, og_cols(2)], og.at[2, first], at_z(2)),
            send(og_in.at[second, og_cols(2)], og.at[2, second], at_z(-2)),
        ),
    ]

    def lanes_of(j):
        xs = lax.rem(x + 4 + j, 4)
        return pl.ds(pl.multiple_of((lax.div(xs, 2) * 5 + lax.rem(xs, 2) * 3) * 128, 128), 256)

    def main_part(j, n, part, parts):
        size = size_of(n) // parts
        return wfull.at[pl.ds(384 * n + part * size, size), lanes_of(j)]

    def rest_part(j, n, part, parts):
        size = (192 if n < 3 else 256) // parts
        return wrecv.at[lax.rem(x + 4 + j, 4), pl.ds(192 * n + part * size, size)]

    def place(src, dst):
        dst[0:25, 0:DROW] = src[...].astype(F32)
        value = dst[:, 0:384]
        main = jnp.where(odd == 1, pltpu.roll(value, 320, 1), value)[:, :256]
        rest = jnp.where(odd == 1, value[:, :128], value[:, 256:])
        dst[:, 0:256] = main
        dst[:, 256:384] = rest
        dst[:, 384:512] = pltpu.roll(rest, 64, 1)

    def rest_of(src, g):
        here, after = src[pl.ds(g, 1), :], src[pl.ds(g + 1, 1), :]
        left, right = jnp.where(odd == 1, after, here), jnp.where(odd == 1, here, after)
        return jnp.where(low[:1], left[:, 256:384], right[:, 384:512])

    low = lax.broadcasted_iota(jnp.int32, (64, 128), 1) < 64
    main_rows = pl.ds(pl.multiple_of(odd * 64, 64), 256)
    rest_rows = pl.ds(pl.multiple_of(256 - odd * 256, 64), 64)

    def weight_tile(i, width):
        at = pl.ds(i * 128, width) if isinstance(i, int) else pl.ds(pl.multiple_of(i * 128, 128), width)
        main = codes[main_rows, at].astype(F32).T
        rest = codes[rest_rows, at].astype(F32)
        if width == 128:
            turned = pltpu.roll(rest, 64, 1)
            stack = jnp.where(odd == 1, jnp.concatenate([turned, rest]), jnp.concatenate([rest, turned]))
            packed = stack.T[:64]
        else:
            packed = jnp.concatenate([rest, rest]).T
        for k in range(width // 64):
            g = 2 * i + k
            value = (main[64 * k : 64 * k + 64] - zps[pl.ds(g, 1), 0:256]) * scs[pl.ds(g, 1), 0:256]
            wfull[pl.ds(i * 128 + 64 * k if isinstance(i, int) else pl.multiple_of(i * 128 + 64 * k, 64), 64), lanes_of(0)] = value.astype(BF16)
        if width == 128:
            zp, sc = rest_of(zps, 2 * i), rest_of(scs, 2 * i)
        else:
            zp, sc = (jnp.where(low[:1], a[24:25, 256:384], a[24:25, 384:512]) for a in (zps, scs))
        wrecv[x, pl.ds(i * 64 if isinstance(i, int) else pl.multiple_of(i * 64, 64), 64), :] = ((packed - zp) * sc).astype(BF16)

    w_plus, w_minus, w_two = {}, {}, {}

    def weights(n):
        def step(i, _):
            weight_tile(3 * n + i, 128)
            return 0

        lax.fori_loop(0, 3, step, 0)
        if n == 3:
            weight_tile(12, 64)
        for kept, k in ((w_plus, 1), (w_minus, -1)):
            kept[n] = [send(part(0, n, 0, 1), part(0, n, 0, 1), at_x(k)) for part in (main_part, rest_part)]

    def weights_on(n):
        for copy in w_plus[n]:
            copy.wait_recv()
        w_two[n] = [send(part(-1, n, 0, 2), part(-1, n, 0, 2), at_x(1)) for part in (main_part, rest_part)]
        for copy in w_minus[n]:
            copy.wait_recv()
        w_two[n] += [send(part(1, n, 1, 2), part(1, n, 1, 2), at_x(-1)) for part in (main_part, rest_part)]

    def unpack(n):
        for i in range(3 * n, 3 * n + (3 if n < 3 else 4)):
            for pair in range(2):
                even = wrecv[2 * pair, pl.ds(64 * i, 64), :].astype(F32)
                next_ = wrecv[2 * pair + 1, pl.ds(64 * i, 64), :].astype(F32)
                lanes = pl.ds((pair * 5 + 2) * 128, 128)
                wfull[pl.ds(128 * i, 64), lanes] = jnp.where(low, even, next_).astype(BF16)
                if i < 12:
                    turned = pltpu.roll(jnp.where(low, next_, even), 64, 1)
                    wfull[pl.ds(128 * i + 64, 64), lanes] = turned.astype(BF16)

    def hidden_rows(i, _):
        rows = pl.ds(pl.multiple_of(i * 320, 16), 320)
        gate = g_v[rows, :].astype(F32)
        up = u_v[rows, :].astype(F32)
        sig = 1.0 / (1.0 + jnp.exp(-gate))
        gs = gate * sig
        m_buf[rows, :] = (gs * up).astype(BF16)
        a1[rows, :] = up * sig * (1.0 + gate * (1.0 - sig))
        a2[rows, :] = gs
        return 0

    def mixed(n):
        part = jnp.dot(hid[...], rot[:, 384 * n : 384 * n + size_of(n)], preferred_element_type=F32)
        mix[0, rows_of(n), :] = part.T.astype(BF16)

    sign_c = jnp.where(c == 1, -1.0, 1.0).astype(F32)
    over_core, over_y, over_back = {}, {}, {}
    dst_of = (h_buf, g_buf)

    def part_at(n, i):
        size = size_of(n) // 4
        return pl.ds(pl.multiple_of(384 * n + i * size, 16), size)

    def had1(slot, n):
        over_core[slot, n] = send(mix.at[slot, rows_of(n)], c_buf.at[slot, rows_of(n)], other)

    def had2(slot, n):
        over_core[slot, n].wait_recv()
        rows, few = rows_of(n), pl.ds(96 * n, size_of(n) // 4)
        mine = mix[slot, rows, :].astype(F32) * sign_c + c_buf[slot, rows, :].astype(F32)
        m2 = mix.at[2 + slot]
        m2[rows, :] = mine.astype(BF16)
        over_y[slot, n] = [
            send(m2.at[part_at(n, lax.rem(y + k, 4))], yv.at[slot, y, few], at_y(k)) for k in (2, 1, 3)
        ]
        yv[slot, y, few, :] = m2[part_at(n, y), :]

    def had3(slot, n):
        for copy in over_y[slot, n]:
            copy.wait_recv()
        few = pl.ds(96 * n, size_of(n) // 4)
        v = [yv[slot, i, few, :].astype(F32) for i in range(4)]
        p0, p1, n0, n1 = v[0] + v[1], v[2] + v[3], v[0] - v[1], v[2] - v[3]
        scale = 0.25 if slot else 1.0
        for i, value in enumerate((p0 + p1, n0 + n1, p0 - p1, n0 - n1)):
            yo[slot, i, few, :] = (value * scale).astype(BF16)
        dst = dst_of[slot]
        over_back[slot, n] = [
            send(yo.at[slot, lax.rem(y + k, 4), few], dst.at[part_at(n, y)], at_y(k)) for k in (2, 1, 3)
        ]
        dst[part_at(n, y), :] = yo[slot, y, few, :]

    def had4(slot, n):
        for copy in over_back[slot, n]:
            copy.wait_recv()

    got_p, got_m = {}, {}

    def ag(k, n):
        rows = rows_of(n)
        if k == 1:
            had4(0, n)
            got_p[1, n] = send(h_buf.at[rows], fp.at[0, rows], at_z(1))
            got_m[1, n] = send(h_buf.at[rows], fm.at[0, rows], at_z(-1))
            return
        got_p[k - 1, n].wait_recv()
        if k < 4 or n in HALF_A:
            got_p[k, n] = send(fp.at[k - 2, rows], fp.at[k - 1, rows], at_z(1))
        got_m[k - 1, n].wait_recv()
        if k < 4 or n in HALF_B:
            got_m[k, n] = send(fm.at[k - 2, rows], fm.at[k - 1, rows], at_z(-1))

    og_all = og.reshape(4 * TOK, DG)

    def grad_part(n):
        for copy in w_two[n]:
            copy.wait_recv()
        unpack(n)
        rows = rows_of(n)
        part = lax.dot_general(
            wfull[rows, :], og_all[...], (((1,), (1,)), ((), ())), preferred_element_type=F32
        )
        for k in range(4):
            pk[k, rows, :] = part[:, k * TOK : (k + 1) * TOK]

    def sign_of(at):
        far = lax.div(lax.rem(pos + 8 + at, 8), 4)
        return jnp.where(far * zh == 1, -1.0, 1.0).astype(F32)

    sum_p, sum_m = {}, {}

    def send_sum(up, d, n):
        rows = rows_of(n)
        kept, got, out, way = (sum_p, rp, sp, 1) if up else (sum_m, rm, sm, -1)
        value = pk[way * d % 4, rows, :] * sign_of(way * d)
        if (d, n) in kept:
            kept[d, n].wait_recv()
            value = value + got[d, rows, :].astype(F32)
        out[d - 1, rows, :] = value.astype(BF16)
        kept[d - 1, n] = send(out.at[d - 1, rows], got.at[d - 1, rows], at_z(way))

    def rs(step, n):
        long_up = n in HALF_A
        for up in (long_up, not long_up):
            d = (4 if up == long_up else 3) - step
            if d >= 1:
                send_sum(up, d, n)

    def rs_end(n):
        rows = rows_of(n)
        sum_p[0, n].wait_recv()
        sum_m[0, n].wait_recv()
        value = pk[0, rows, :] * sign_of(0)
        value = value + rp[0, rows, :].astype(F32) + rm[0, rows, :].astype(F32)
        mix[1, rows, :] = value.astype(BF16)
        had1(1, n)

    def rotated(n):
        rows = rows_of(n)
        (got_p if n in HALF_A else got_m)[4, n].wait_recv()
        for k in range(4):
            mine = h_buf if k == 0 else fm.at[k - 1]
            far = fp.at[3 - k] if k else (fp if n in HALF_A else fm).at[3]
            value = mine[rows, :].astype(F32) * (sign_of(k) * 0.25)
            value = value + far[rows, :].astype(F32) * (sign_of(k + 4) * 0.25)
            rott[rows, pl.ds(k * TOK, TOK)] = value.astype(BF16)

    def weight_grad(n):
        rows, groups = rows_of(n), size_of(n) // 64
        part = jnp.dot(rott[rows, :], og_all[...], preferred_element_type=F32)
        part = part * wfull[rows, :].astype(F32)
        s3[n, 0:groups, :] = jnp.sum(part.reshape(groups, 64, DG), axis=1)

    def s_lanes(j):
        xs = lax.rem(x + 4 + j, 4)
        return pl.ds(pl.multiple_of((lax.div(xs, 2) * 5 + lax.rem(xs, 2) * 2) * 128, 128), 384)

    place(zp_in, zps)
    place(sc_in, scs)
    loads[0].wait()
    weights(0)
    loads[1].wait()
    loads[2].wait()
    lax.fori_loop(0, 5, hidden_rows, 0)
    hid[...] = m_buf[...].astype(F32).T.astype(BF16)
    loads[3].wait()
    mixed(0)
    had1(0, 0)
    weights(1)
    mixed(1)
    had1(0, 1)
    had2(0, 0)
    mixed(2)
    had1(0, 2)
    had2(0, 1)
    had3(0, 0)
    weights(2)
    mixed(3)
    had1(0, 3)
    had2(0, 2)
    had3(0, 1)
    weights_on(0)
    weights(3)
    ag(1, 0)
    had2(0, 3)
    had3(0, 2)
    ag(1, 1)
    og_near = []
    for k, copies in zip((3, 1, 2), og_far):
        for copy in copies:
            copy.wait_recv()
        og_near.append(send(og.at[k, half], og.at[k, half], other))
    had3(0, 3)
    ag(1, 2)
    weights_on(1)
    ag(1, 3)
    loads[4].wait()
    for copy in og_near:
        copy.wait_recv()
    s3[...] = jnp.zeros_like(s3)
    grad_part(0)
    rs(0, 0)
    ag(2, 0)
    ag(2, 1)
    weights_on(2)
    rs(1, 0)
    grad_part(1)
    rs(0, 1)
    ag(2, 2)
    rs(2, 0)
    ag(2, 3)
    rs(1, 1)
    weights_on(3)
    grad_part(2)
    rs(0, 2)
    rs(3, 0)
    ag(3, 0)
    rs(2, 1)
    rs(1, 2)
    ag(3, 1)
    rs_end(0)
    grad_part(3)
    rs(0, 3)
    rs(3, 1)
    had2(1, 0)
    rs(2, 2)
    ag(3, 2)
    rs(1, 3)
    had3(1, 0)
    rs_end(1)
    rs(3, 2)
    ag(3, 3)
    had2(1, 1)
    rs(2, 3)
    ag(4, 0)
    rs_end(2)
    had3(1, 1)
    rs(3, 3)
    ag(4, 1)
    had2(1, 2)
    ag(4, 2)
    ag(4, 3)
    had3(1, 2)
    rotated(0)
    weight_grad(0)
    rs_end(3)
    rotated(1)
    weight_grad(1)
    had2(1, 3)
    rotated(2)
    weight_grad(2)
    had3(1, 3)
    rotated(3)
    weight_grad(3)
    ls_copies = [
        send(s3.at[:, :, s_lanes(j)], lsb.at[j - 1], at_x(j)) for j in (1, 2, 3)
    ]
    for n in range(4):
        had4(1, n)

    def last_rows(i, _):
        rows = pl.ds(pl.multiple_of(i * 320, 16), 320)
        grad = jnp.dot(rot[rows, :], g_buf[...], preferred_element_type=F32)
        o_gg[rows, :] = (grad * a1[rows, :]).astype(BF16)
        o_gu[rows, :] = (grad * a2[rows, :]).astype(BF16)
        return 0

    lax.fori_loop(0, 5, last_rows, 0)
    for copy in ls_copies:
        copy.wait_recv()
    total = s3[:, :, s_lanes(0)]
    for j in range(3):
        total = total + lsb[j]
    total = total.reshape(32, 384)
    total = jnp.where(odd == 1, pltpu.roll(total, 320, 1), total)[:, :DROW]
    for n in range(4):
        groups = size_of(n) // 64
        o_ls[6 * n : 6 * n + groups, :] = total[8 * n : 8 * n + groups, :]
    for copy in pending:
        copy.wait_send()


def on_device(out_grad, gate_act, up_act, codes, zero_points, scales, rotation):
    vm = pl.BlockSpec(memory_space=pltpu.VMEM)
    hbm = pl.BlockSpec(memory_space=pl.ANY)
    gg, gu, ls = pl.pallas_call(
        kernel,
        out_shape=(
            jax.ShapeDtypeStruct((BLK, TOK), BF16),
            jax.ShapeDtypeStruct((BLK, TOK), BF16),
            jax.ShapeDtypeStruct((25, DROW), F32),
        ),
        in_specs=[hbm, hbm, hbm, hbm, vm, vm, hbm],
        out_specs=(vm, vm, vm),
        scratch_shapes=[
            pltpu.VMEM((DROW, BLK), jnp.int32),
            pltpu.VMEM((BLK, BLK), BF16),
            pltpu.VMEM((BLK, TOK), BF16),
            pltpu.VMEM((BLK, TOK), BF16),
            pltpu.VMEM((BLK, DG), BF16),
            pltpu.VMEM((4, REST, 128), BF16),
            pltpu.VMEM((4, TOK, DG), BF16),
            pltpu.VMEM((TOK, BLK), BF16),
            pltpu.VMEM((BLK, TOK), BF16),
            pltpu.VMEM((2, BLK, TOK), BF16),
            pltpu.VMEM((4, BLK, TOK), BF16),
            pltpu.VMEM((2, 4, BLK // 4, TOK), BF16),
            pltpu.VMEM((2, 4, BLK // 4, TOK), BF16),
            pltpu.VMEM((BLK, TOK), BF16),
            pltpu.VMEM((4, BLK, TOK), BF16),
            pltpu.VMEM((4, BLK, TOK), BF16),
            pltpu.VMEM((BLK, 4 * TOK), BF16),
            pltpu.VMEM((4, BLK, TOK), F32),
            pltpu.VMEM((4, BLK, TOK), BF16),
            pltpu.VMEM((4, BLK, TOK), BF16),
            pltpu.VMEM((4, BLK, TOK), BF16),
            pltpu.VMEM((4, BLK, TOK), BF16),
            pltpu.VMEM((BLK, TOK), BF16),
            pltpu.VMEM((BLK, TOK), F32),
            pltpu.VMEM((BLK, TOK), F32),
            pltpu.VMEM((4, 8, DG), F32),
            pltpu.VMEM((3, 4, 8, 384), F32),
            pltpu.VMEM((32, 512), F32),
            pltpu.VMEM((32, 512), F32),
            pltpu.SemaphoreType.DMA((5,)),
            pltpu.SemaphoreType.DMA((N_COPY,)),
            pltpu.SemaphoreType.DMA((N_COPY,)),
        ],
        name="whole",
        compiler_params=pltpu.CompilerParams(
            collective_id=0, has_side_effects=True, vmem_limit_bytes=56 << 20
        ),
    )(out_grad, gate_act.T, up_act.T, codes, zero_points.T, scales.T, rotation)
    return gg.T, gu.T, ls.T


def solution(mesh):
    return jax.shard_map(
        on_device,
        mesh=mesh,
        in_specs=(
            P("dp", None),
            P("dp", "tensor"),
            P("dp", "tensor"),
            P("dp", "tensor"),
            P("dp", "tensor"),
            P("dp", "tensor"),
            P(),
        ),
        out_specs=(P("dp", "tensor"), P("dp", "tensor"), P("dp", "tensor")),
        check_vma=False,
    )
```

time: 401 us -> 107 us (0.27); the launches traced: 395 us -> 106 us
  waiting for transfers between devices: 197 us -> 0 us
  Pallas kernels: 0 us -> 100 us
  blocking collectives: 64.5 us -> 0 us
  local copies, waits for them, and re-layouts: 49 us -> 4.98 us
  matrix products: 28 us -> 0 us
  other arithmetic: 25.3 us -> 0 us
  starting transfers between devices: 16.4 us -> 0 us
  between operations: 14.6 us -> 0.64 us
    pallas_call x0 -> x1, Pallas kernels: none -> 100 us  [on_device(): pl.pallas_call(kernel, out_shape=(jax.ShapeDtypeStruct((BLK, TOK), BF16),...]
    all_gather x1 -> x0, waiting for transfers between devices: 91.9 us -> none  [on_device(): lax.all_gather(rotated, 'dp', axis=0, tiled=True)]
    reduce_scatter x1 -> x0, waiting for transfers between devices: 79.6 us -> none  [on_device(): lax.psum_scatter(jnp.dot(grad_slice, weight, preferred_element_type=jnp.f...]
    all_to_all x3 -> x0, blocking collectives: 64.5 us -> none  [the longest x2 43.2 us: spread(): lax.all_to_all(stacked, 'tensor', split_axis=3, concat_axis=0, tiled=True)]
    dot_general x6 -> x0, matrix products: 28 us -> none  [the longest x1 9.91 us: on_device(): jnp.dot(grad_slice, weight, preferred_element_type=jnp.float32)]
    all_to_all x2 -> x0, waiting for transfers between devices: 25.5 us -> none  [the longest x1 25.5 us: on_device(): lax.all_to_all(out_grad, 'dp', split_axis=1, concat_axis=0, tiled=True)]
    unnamed x2 -> x0, other arithmetic: 19.8 us -> none
    all_to_all x4 -> x0, local copies, waits for them, and re-layouts: 17.3 us -> none  [spread(): lax.all_to_all(stacked, 'tensor', split_axis=3, concat_axis=0, tiled=True)]
  transfers between devices with their start and end apart: 4 -> 0, of which waited for: 3 -> 0; matrix products, arithmetic and copies ran while one was open for 21% -> 0% of each run, Pallas kernels for 0% -> 0%
where the time goes in v2:
time: 107 us; the launch traced here: 106 us
  Pallas kernels  100 us (93%)
  local copies, waits for them, and re-layouts  4.98 us (5%)
    pallas_call x1, Pallas kernels, on_device(): pl.pallas_call(kernel, out_shape=(jax.ShapeDtypeStruct((BLK, TOK), BF16),...  100 us
    unnamed x3, local copies, waits for them, and re-layouts  4.98 us

profile of v2, /device:TPU:8, one launch (start us, length us, event | category | flops | bytes accessed | tf_op | source)
XLA Modules:
  0.0 105.8 jit_solution(7951755048944901715)
XLA Ops:
  0.6 100.2 %whole.1 = (bf16[1600,128]{1,0:T(8,128)(2,1)}, bf16[1600,128]{1,0:T(8,128)(2,1)}, f32[25,320]{1,0:T(8,128)}) custom-call(bf16[128,5120]{1,0:T(8,128)(2,1)} %og_in.1, bf16[1600,128]{1,0:T(8,128)(2,1)} %bitcast.9, bf16[1600,128]{1,0:T(8,128)(2,1)} %bitcast.10, s32[320,1600]{1,0:T(8,128)} %codes_in.1, s32[25,320]{1,0:T(8,128)} %bitcast.11, f32[25,320]{1,0:T(8,128)} %bitcast.12, ...), custom_call_target="tpu_custom_call" | custom-call | tf_op jit(solution)/shard_map/whole/pallas_call | solution.py:444
  100.8 1.8 %copy.13 = bf16[128,1600]{0,1:T(8,128)(2,1)} copy(bf16[128,1600]{0,1:T(8,128)(2,1)} %bitcast.8) | data formatting | bytes 819200
  102.6 1.8 %copy.14 = bf16[128,1600]{0,1:T(8,128)(2,1)} copy(bf16[128,1600]{0,1:T(8,128)(2,1)} %bitcast.7) | data formatting | bytes 819200
  104.4 1.4 %copy.15 = f32[320,25]{0,1:T(8,128)} copy(f32[320,25]{0,1:T(8,128)} %bitcast.13) | data formatting | bytes 64000

commit v3 on v2

--- a/solution.py
+++ b/solution.py
@@ -14,8 +14,22 @@
 DG = 1280
 REST = 832
 HALF_A, HALF_B = (0, 2), (1, 3)
-N_COPY = 154
-
+N_COPY = 178
+
+
+ORDER = (
+    ("hidden",), ("mixed", 0), ("mixed", 1), ("weights", 0), ("had3", 0, 0), ("mixed", 2), ("mixed", 3),
+    ("had3", 0, 1), ("weights", 1), ("ag", 1, 0), ("had3", 0, 2), ("weights_on", 0), ("weights", 2), ("had3", 0, 3),
+    ("ag", 2, 0), ("ag", 1, 1), ("og_on",), ("ag", 1, 2), ("weights_on", 1), ("weights", 3), ("ag", 1, 3),
+    ("grad_part", 0), ("rs", 0, 0), ("ag", 2, 1), ("ag", 2, 2), ("weights_on", 2), ("rs", 1, 0), ("grad_part", 1),
+    ("rs", 0, 1), ("ag", 3, 1), ("rs", 2, 0), ("rs", 1, 1), ("weights_on", 3), ("ag", 4, 1), ("grad_part", 2),
+    ("rs", 0, 2), ("rs", 3, 0), ("rs", 2, 1), ("grad_part", 3), ("rs", 0, 3), ("rotated", 1), ("weight_grad", 1),
+    ("rs", 1, 2), ("rs_end", 0), ("rs", 3, 1), ("ag", 2, 3), ("rs", 1, 3), ("had3", 1, 0), ("rs", 2, 2),
+    ("rs_end", 1), ("last_part", 0), ("ag", 3, 2), ("rs", 2, 3), ("had3", 1, 1), ("rs", 3, 2), ("ag", 3, 3),
+    ("last_part", 1), ("ag", 3, 0), ("rs", 3, 3), ("rs_end", 2), ("ag", 4, 2), ("ag", 4, 3), ("ag", 4, 0),
+    ("had3", 1, 2), ("rs_end", 3), ("rotated", 2), ("weight_grad", 2), ("rotated", 3), ("weight_grad", 3),
+    ("rotated", 0), ("weight_grad", 0), ("ls_send",), ("had3", 1, 3), ("last_part", 2), ("ls_end",), ("last_part", 3),
+)
 
 def rows_of(n):
     return pl.ds(384 * n, size_of(n))
@@ -27,9 +41,9 @@
 
 def kernel(
     og_in, g_in, u_in, codes_in, zp_in, sc_in, rot_in,
-    o_gg, o_gu, o_ls,
-    codes, rot, g_v, u_v, wfull, wrecv, og, hid, m_buf, c_buf, mix, yv, yo, h_buf, fp, fm, rott, pk,
-    sp, sm, rp, rm, g_buf, a1, a2, s3, lsb, zps, scs, lsem, ssem, rsem,
+    o_gh, o_ls,
+    codes, rot, g_v, u_v, wfull, wrecv, og, hid, m_buf, mix, yv, yo, h_buf, fp, fm, rott, pk,
+    sp, sm, rp, rm, g_buf, s3, lsb, z_v, s_v, zps, scs, lsem, ssem, rsem,
 ):
     dp = lax.axis_index("dp")
     tn = lax.axis_index("tensor")
@@ -44,23 +58,33 @@
     def at_y(k):
         return (dp, lax.rem(y + 4 + k, 4) * 4 + zh * 2 + c)
 
+    def across(k):
+        return (dp, lax.rem(y + 4 + k, 4) * 4 + zh * 2 + 1 - c)
+
     def at_z(k):
         to = lax.rem(pos + 8 + k, 8)
         return (lax.rem(to, 4) * 4 + x, y * 4 + lax.div(to, 4) * 2 + c)
 
-    other = (dp, y * 4 + zh * 2 + 1 - c)
+    other = across(0)
 
     def og_cols(k):
         return pl.ds(pl.multiple_of(lax.rem(zl + 4 + k, 4) * DG, 128), DG)
 
-    loads = [
-        pltpu.make_async_copy(src, dst, lsem.at[i])
-        for i, (src, dst) in enumerate(
-            ((codes_in, codes), (g_in, g_v), (u_in, u_v), (rot_in, rot), (og_in.at[:, og_cols(0)], og.at[0]))
-        )
-    ]
-    for load in loads:
-        load.start()
+    moves = {"gate": (g_in, g_v), "up": (u_in, u_v), "zp": (zp_in, z_v), "sc": (sc_in, s_v)}
+    for n in range(4):
+        cols = rows_of(n)
+        moves["rot", n] = (rot_in.at[:, cols], rot.at[:, cols])
+        moves["codes", n] = (codes_in.at[:, cols], codes.at[:, cols])
+    moves["og"] = (og_in.at[:, og_cols(0)], og.at[0])
+    loads = {
+        name: pltpu.make_async_copy(src, dst, lsem.at[i])
+        for i, (name, (src, dst)) in enumerate(moves.items())
+    }
+    def load(*names):
+        for name in names:
+            loads[name].start()
+
+    load("gate", "up", ("rot", 0))
 
     count = [0]
     pending = []
@@ -78,21 +102,22 @@
 
     barrier = pltpu.get_barrier_semaphore()
     peers = [at_x(1), at_x(2), at_x(3), at_y(1), at_y(2), at_y(3)]
-    peers += [at_z(1), at_z(-1), at_z(2), at_z(-2), other]
+    peers += [at_z(1), at_z(-1), at_z(2), at_z(-2), other, across(1), across(2), across(3)]
     for peer in peers:
         pl.semaphore_signal(barrier, inc=1, device_id=peer, device_id_type=MESH)
     pl.semaphore_wait(barrier, len(peers))
 
     half = pl.ds(pl.multiple_of(c * 64, 64), 64)
     first, second = (pl.ds(pl.multiple_of(c * 64 + i * 32, 32), 32) for i in (0, 1))
-    og_far = [
-        (send(og_in.at[half, og_cols(1)], og.at[3, half], at_z(1)),),
-        (send(og_in.at[half, og_cols(-1)], og.at[1, half], at_z(-1)),),
-        (
+    og_far = []
+
+    def og_start():
+        og_far.append((send(og_in.at[half, og_cols(1)], og.at[3, half], at_z(1)),))
+        og_far.append((send(og_in.at[half, og_cols(-1)], og.at[1, half], at_z(-1)),))
+        og_far.append((
             send(og_in.at[first, og_cols(2)], og.at[2, first], at_z(2)),
             send(og_in.at[second, og_cols(2)], og.at[2, second], at_z(-2)),
-        ),
-    ]
+        ))
 
     def lanes_of(j):
         xs = lax.rem(x + 4 + j, 4)
@@ -151,6 +176,12 @@
             weight_tile(3 * n + i, 128)
             return 0
 
+        if n == 0:
+            loads["zp"].wait()
+            loads["sc"].wait()
+            place(z_v, zps)
+            place(s_v, scs)
+        loads["codes", n].wait()
         lax.fori_loop(0, 3, step, 0)
         if n == 3:
             weight_tile(12, 64)
@@ -180,44 +211,48 @@
         rows = pl.ds(pl.multiple_of(i * 320, 16), 320)
         gate = g_v[rows, :].astype(F32)
         up = u_v[rows, :].astype(F32)
-        sig = 1.0 / (1.0 + jnp.exp(-gate))
-        gs = gate * sig
-        m_buf[rows, :] = (gs * up).astype(BF16)
-        a1[rows, :] = up * sig * (1.0 + gate * (1.0 - sig))
-        a2[rows, :] = gs
+        m_buf[rows, :] = (gate * (1.0 / (1.0 + jnp.exp(-gate))) * up).astype(BF16)
         return 0
 
+    def hidden():
+        loads["gate"].wait()
+        loads["up"].wait()
+        lax.fori_loop(0, 5, hidden_rows, 0)
+        hid[...] = m_buf[...].astype(F32).T.astype(BF16)
+        load(("codes", 0), "zp", "sc", ("rot", 1))
+
     def mixed(n):
+        loads["rot", n].wait()
         part = jnp.dot(hid[...], rot[:, 384 * n : 384 * n + size_of(n)], preferred_element_type=F32)
         mix[0, rows_of(n), :] = part.T.astype(BF16)
+        had2(0, n)
+        if n == 0:
+            load(("rot", 2), ("rot", 3))
+            og_start()
+        elif n == 1:
+            load(("codes", 1), ("codes", 2), ("codes", 3), "og")
 
     sign_c = jnp.where(c == 1, -1.0, 1.0).astype(F32)
-    over_core, over_y, over_back = {}, {}, {}
+    over_y, over_back = {}, {}
     dst_of = (h_buf, g_buf)
 
     def part_at(n, i):
         size = size_of(n) // 4
         return pl.ds(pl.multiple_of(384 * n + i * size, 16), size)
 
-    def had1(slot, n):
-        over_core[slot, n] = send(mix.at[slot, rows_of(n)], c_buf.at[slot, rows_of(n)], other)
-
     def had2(slot, n):
-        over_core[slot, n].wait_recv()
-        rows, few = rows_of(n), pl.ds(96 * n, size_of(n) // 4)
-        mine = mix[slot, rows, :].astype(F32) * sign_c + c_buf[slot, rows, :].astype(F32)
-        m2 = mix.at[2 + slot]
-        m2[rows, :] = mine.astype(BF16)
+        src, few = mix.at[slot], pl.ds(96 * n, size_of(n) // 4)
         over_y[slot, n] = [
-            send(m2.at[part_at(n, lax.rem(y + k, 4))], yv.at[slot, y, few], at_y(k)) for k in (2, 1, 3)
+            send(src.at[part_at(n, lax.rem(y + k, 4))], yv.at[slot, 4 * c + y, few], to(k))
+            for to, k in ((across, 2), (at_y, 2), (across, 1), (at_y, 1), (across, 3), (at_y, 3), (across, 0))
         ]
-        yv[slot, y, few, :] = m2[part_at(n, y), :]
+        yv[slot, 4 * c + y, few, :] = src[part_at(n, y), :]
 
     def had3(slot, n):
         for copy in over_y[slot, n]:
             copy.wait_recv()
         few = pl.ds(96 * n, size_of(n) // 4)
-        v = [yv[slot, i, few, :].astype(F32) for i in range(4)]
+        v = [yv[slot, i, few, :].astype(F32) + yv[slot, 4 + i, few, :].astype(F32) * sign_c for i in range(4)]
         p0, p1, n0, n1 = v[0] + v[1], v[2] + v[3], v[0] - v[1], v[2] - v[3]
         scale = 0.25 if slot else 1.0
         for i, value in enumerate((p0 + p1, n0 + n1, p0 - p1, n0 - n1)):
@@ -249,8 +284,19 @@
             got_m[k, n] = send(fm.at[k - 2, rows], fm.at[k - 1, rows], at_z(-1))
 
     og_all = og.reshape(4 * TOK, DG)
+    og_near = []
+
+    def og_on():
+        for k, copies in zip((3, 1, 2), og_far):
+            for copy in copies:
+                copy.wait_recv()
+            og_near.append(send(og.at[k, half], og.at[k, half], other))
 
     def grad_part(n):
+        while og_near:
+            og_near.pop().wait_recv()
+            if not og_near:
+                loads["og"].wait()
         for copy in w_two[n]:
             copy.wait_recv()
         unpack(n)
@@ -291,7 +337,7 @@
         value = pk[0, rows, :] * sign_of(0)
         value = value + rp[0, rows, :].astype(F32) + rm[0, rows, :].astype(F32)
         mix[1, rows, :] = value.astype(BF16)
-        had1(1, n)
+        had2(1, n)
 
     def rotated(n):
         rows = rows_of(n)
@@ -307,149 +353,75 @@
         rows, groups = rows_of(n), size_of(n) // 64
         part = jnp.dot(rott[rows, :], og_all[...], preferred_element_type=F32)
         part = part * wfull[rows, :].astype(F32)
+        s3[n, 6:8, :] = jnp.zeros((2, DG), F32)
         s3[n, 0:groups, :] = jnp.sum(part.reshape(groups, 64, DG), axis=1)
 
     def s_lanes(j):
         xs = lax.rem(x + 4 + j, 4)
         return pl.ds(pl.multiple_of((lax.div(xs, 2) * 5 + lax.rem(xs, 2) * 2) * 128, 128), 384)
 
-    place(zp_in, zps)
-    place(sc_in, scs)
-    loads[0].wait()
-    weights(0)
-    loads[1].wait()
-    loads[2].wait()
-    lax.fori_loop(0, 5, hidden_rows, 0)
-    hid[...] = m_buf[...].astype(F32).T.astype(BF16)
-    loads[3].wait()
-    mixed(0)
-    had1(0, 0)
-    weights(1)
-    mixed(1)
-    had1(0, 1)
-    had2(0, 0)
-    mixed(2)
-    had1(0, 2)
-    had2(0, 1)
-    had3(0, 0)
-    weights(2)
-    mixed(3)
-    had1(0, 3)
-    had2(0, 2)
-    had3(0, 1)
-    weights_on(0)
-    weights(3)
-    ag(1, 0)
-    had2(0, 3)
-    had3(0, 2)
-    ag(1, 1)
-    og_near = []
-    for k, copies in zip((3, 1, 2), og_far):
-        for copy in copies:
-            copy.wait_recv()
-        og_near.append(send(og.at[k, half], og.at[k, half], other))
-    had3(0, 3)
-    ag(1, 2)
-    weights_on(1)
-    ag(1, 3)
-    loads[4].wait()
-    for copy in og_near:
-        copy.wait_recv()
-    s3[...] = jnp.zeros_like(s3)
-    grad_part(0)
-    rs(0, 0)
-    ag(2, 0)
-    ag(2, 1)
-    weights_on(2)
-    rs(1, 0)
-    grad_part(1)
-    rs(0, 1)
-    ag(2, 2)
-    rs(2, 0)
-    ag(2, 3)
-    rs(1, 1)
-    weights_on(3)
-    grad_part(2)
-    rs(0, 2)
-    rs(3, 0)
-    ag(3, 0)
-    rs(2, 1)
-    rs(1, 2)
-    ag(3, 1)
-    rs_end(0)
-    grad_part(3)
-    rs(0, 3)
-    rs(3, 1)
-    had2(1, 0)
-    rs(2, 2)
-    ag(3, 2)
-    rs(1, 3)
-    had3(1, 0)
-    rs_end(1)
-    rs(3, 2)
-    ag(3, 3)
-    had2(1, 1)
-    rs(2, 3)
-    ag(4, 0)
-    rs_end(2)
-    had3(1, 1)
-    rs(3, 3)
-    ag(4, 1)
-    had2(1, 2)
-    ag(4, 2)
-    ag(4, 3)
-    had3(1, 2)
-    rotated(0)
-    weight_grad(0)
-    rs_end(3)
-    rotated(1)
-    weight_grad(1)
-    had2(1, 3)
-    rotated(2)
-    weight_grad(2)
-    had3(1, 3)
-    rotated(3)
-    weight_grad(3)
-    ls_copies = [
-        send(s3.at[:, :, s_lanes(j)], lsb.at[j - 1], at_x(j)) for j in (1, 2, 3)
-    ]
-    for n in range(4):
+    ls_copies = []
+
+    def ls_send():
+        ls_copies.extend(send(s3.at[:, :, s_lanes(j)], lsb.at[j - 1], at_x(j)) for j in (1, 2, 3))
+
+    def ls_end():
+        for copy in ls_copies:
+            copy.wait_recv()
+        total = s3[:, :, s_lanes(0)]
+        for j in range(3):
+            total = total + lsb[j]
+        total = total.reshape(32, 384)
+        o_ls[...] = jnp.where(odd == 1, pltpu.roll(total, 320, 1), total)[:, :DROW]
+
+    summed = []
+
+    def last_part(n):
         had4(1, n)
-
-    def last_rows(i, _):
-        rows = pl.ds(pl.multiple_of(i * 320, 16), 320)
-        grad = jnp.dot(rot[rows, :], g_buf[...], preferred_element_type=F32)
-        o_gg[rows, :] = (grad * a1[rows, :]).astype(BF16)
-        o_gu[rows, :] = (grad * a2[rows, :]).astype(BF16)
-        return 0
-
-    lax.fori_loop(0, 5, last_rows, 0)
-    for copy in ls_copies:
-        copy.wait_recv()
-    total = s3[:, :, s_lanes(0)]
-    for j in range(3):
-        total = total + lsb[j]
-    total = total.reshape(32, 384)
-    total = jnp.where(odd == 1, pltpu.roll(total, 320, 1), total)[:, :DROW]
+        again = bool(summed)
+        summed.append(n)
+
+        def last_rows(i, _):
+            rows = pl.ds(pl.multiple_of(i * 320, 16), 320)
+            grad = jnp.dot(rot[rows, 384 * n : 384 * n + size_of(n)], g_buf[rows_of(n), :], preferred_element_type=F32)
+            o_gh[rows, :] = o_gh[rows, :] + grad if again else grad
+            return 0
+
+        lax.fori_loop(0, 5, last_rows, 0)
+
+    steps = dict(
+        weights=weights, weights_on=weights_on, hidden=hidden, mixed=mixed, had3=had3, ag=ag, rs=rs,
+        og_on=og_on, grad_part=grad_part, rs_end=rs_end, rotated=rotated, weight_grad=weight_grad,
+        ls_send=ls_send, ls_end=ls_end, last_part=last_part,
+    )
+    for name, *at in ORDER:
+        steps[name](*at)
+    for copy in pending:
+        copy.wait_send()
+
+
+def finish(gh, g, u, ls, o_gg, o_gu, o_ls):
+    grad, gate, up = gh[...], g[...].astype(F32), u[...].astype(F32)
+    sig = 1.0 / (1.0 + jnp.exp(-gate))
+    o_gg[...] = (grad * up * sig * (1.0 + gate * (1.0 - sig))).astype(BF16)
+    o_gu[...] = (grad * gate * sig).astype(BF16)
     for n in range(4):
         groups = size_of(n) // 64
-        o_ls[6 * n : 6 * n + groups, :] = total[8 * n : 8 * n + groups, :]
-    for copy in pending:
-        copy.wait_send()
+        o_ls[6 * n : 6 * n + groups, :] = ls[8 * n : 8 * n + groups, :]
 
 
 def on_device(out_grad, gate_act, up_act, codes, zero_points, scales, rotation):
     vm = pl.BlockSpec(memory_space=pltpu.VMEM)
     hbm = pl.BlockSpec(memory_space=pl.ANY)
-    gg, gu, ls = pl.pallas_call(
+    gate_t, up_t = gate_act.T, up_act.T
+    gh, ls = pl.pallas_call(
         kernel,
         out_shape=(
-            jax.ShapeDtypeStruct((BLK, TOK), BF16),
-            jax.ShapeDtypeStruct((BLK, TOK), BF16),
-            jax.ShapeDtypeStruct((25, DROW), F32),
+            jax.ShapeDtypeStruct((BLK, TOK), F32),
+            jax.ShapeDtypeStruct((32, DROW), F32),
         ),
-        in_specs=[hbm, hbm, hbm, hbm, vm, vm, hbm],
-        out_specs=(vm, vm, vm),
+        in_specs=[hbm] * 7,
+        out_specs=(vm, vm),
         scratch_shapes=[
             pltpu.VMEM((DROW, BLK), jnp.int32),
             pltpu.VMEM((BLK, BLK), BF16),
@@ -461,8 +433,7 @@
             pltpu.VMEM((TOK, BLK), BF16),
             pltpu.VMEM((BLK, TOK), BF16),
             pltpu.VMEM((2, BLK, TOK), BF16),
-            pltpu.VMEM((4, BLK, TOK), BF16),
-            pltpu.VMEM((2, 4, BLK // 4, TOK), BF16),
+            pltpu.VMEM((2, 8, BLK // 4, TOK), BF16),
             pltpu.VMEM((2, 4, BLK // 4, TOK), BF16),
             pltpu.VMEM((BLK, TOK), BF16),
             pltpu.VMEM((4, BLK, TOK), BF16),
@@ -474,13 +445,13 @@
             pltpu.VMEM((4, BLK, TOK), BF16),
             pltpu.VMEM((4, BLK, TOK), BF16),
             pltpu.VMEM((BLK, TOK), BF16),
-            pltpu.VMEM((BLK, TOK), F32),
-            pltpu.VMEM((BLK, TOK), F32),
             pltpu.VMEM((4, 8, DG), F32),
             pltpu.VMEM((3, 4, 8, 384), F32),
+            pltpu.VMEM((25, DROW), jnp.int32),
+            pltpu.VMEM((25, DROW), F32),
             pltpu.VMEM((32, 512), F32),
             pltpu.VMEM((32, 512), F32),
-            pltpu.SemaphoreType.DMA((5,)),
+            pltpu.SemaphoreType.DMA((13,)),
             pltpu.SemaphoreType.DMA((N_COPY,)),
             pltpu.SemaphoreType.DMA((N_COPY,)),
         ],
@@ -488,7 +459,20 @@
         compiler_params=pltpu.CompilerParams(
             collective_id=0, has_side_effects=True, vmem_limit_bytes=56 << 20
         ),
-    )(out_grad, gate_act.T, up_act.T, codes, zero_points.T, scales.T, rotation)
+    )(out_grad, gate_t, up_t, codes, zero_points.T, scales.T, rotation)
+    part = pl.BlockSpec((BLK // 2, TOK), lambda i: (i, 0))
+    gg, gu, ls = pl.pallas_call(
+        finish,
+        grid=(2,),
+        out_shape=(
+            jax.ShapeDtypeStruct((BLK, TOK), BF16),
+            jax.ShapeDtypeStruct((BLK, TOK), BF16),
+            jax.ShapeDtypeStruct((25, DROW), F32),
+        ),
+        in_specs=[part, part, part, pl.BlockSpec((32, DROW), lambda i: (0, 0))],
+        out_specs=(part, part, pl.BlockSpec((25, DROW), lambda i: (0, 0))),
+        name="finish",
+    )(gh, gate_t, up_t, ls)
     return gg.T, gu.T, ls.T
 
 

time: 107 us -> 100 us (0.935)
  local copies, waits for them, and re-layouts: 4.98 us -> 0 us
  Pallas kernels: 100 us -> 98.6 us
    unnamed x3 -> x0, local copies, waits for them, and re-layouts: 4.98 us -> none
    pallas_call x1 -> x2, Pallas kernels: 100 us -> 98.6 us  [the longest x1 96.2 us: on_device(): pl.pallas_call(kernel, out_shape=(jax.ShapeDtypeStruct((BLK, TOK), F32),...]
where the time goes in v3:
time: 100 us; the launch traced here: 99.2 us
  Pallas kernels  98.6 us (99%)
    pallas_call x1, Pallas kernels, on_device(): pl.pallas_call(kernel, out_shape=(jax.ShapeDtypeStruct((BLK, TOK), F32),...  96.2 us
    pallas_call x1, Pallas kernels, on_device(): pl.pallas_call(finish, grid=(2,), out_shape=(jax.ShapeDtypeStruct((BLK, T...  2.41 us

profile of v3, /device:TPU:8, one launch (start us, length us, event | category | flops | bytes accessed | tf_op | source)
XLA Modules:
  0.0 99.2 jit_solution(3021462321484740191)
XLA Ops:
  0.6 96.2 %whole.1 = (f32[1600,128]{1,0:T(8,128)}, f32[32,320]{1,0:T(8,128)}) custom-call(bf16[128,5120]{1,0:T(8,128)(2,1)} %og_in.1, bf16[1600,128]{1,0:T(8,128)(2,1)} %bitcast.7, bf16[1600,128]{1,0:T(8,128)(2,1)} %bitcast.9, s32[320,1600]{1,0:T(8,128)} %codes_in.1, s32[25,320]{1,0:T(8,128)} %bitcast.11, f32[25,320]{1,0:T(8,128)} %bitcast.12, bf16[1600,1600]{1,0:T(8,128)(2,1)} %rot_in.1), custom_call_target="tpu_custom_call" | custom-call | tf_op jit(solution)/shard_map/whole/pallas_call | solution.py:417
  96.8 2.4 %finish.1 = (bf16[1600,128]{1,0:T(8,128)(2,1)}, bf16[1600,128]{1,0:T(8,128)(2,1)}, f32[25,320]{1,0:T(8,128)}) custom-call(f32[1600,128]{1,0:T(8,128)} %get-tuple-element.8.gh, bf16[1600,128]{1,0:T(8,128)(2,1)} %bitcast.8, bf16[1600,128]{1,0:T(8,128)(2,1)} %bitcast.10, f32[32,320]{1,0:T(8,128)} %get-tuple-element.9.ls), custom_call_target="tpu_custom_call" | custom-call | tf_op jit(solution)/shard_map/finish/pallas_call | solution.py:464

commit v4 on v3

--- a/solution.py
+++ b/solution.py
@@ -18,17 +18,17 @@
 
 
 ORDER = (
-    ("hidden",), ("mixed", 0), ("mixed", 1), ("weights", 0), ("had3", 0, 0), ("mixed", 2), ("mixed", 3),
-    ("had3", 0, 1), ("weights", 1), ("ag", 1, 0), ("had3", 0, 2), ("weights_on", 0), ("weights", 2), ("had3", 0, 3),
-    ("ag", 2, 0), ("ag", 1, 1), ("og_on",), ("ag", 1, 2), ("weights_on", 1), ("weights", 3), ("ag", 1, 3),
-    ("grad_part", 0), ("rs", 0, 0), ("ag", 2, 1), ("ag", 2, 2), ("weights_on", 2), ("rs", 1, 0), ("grad_part", 1),
-    ("rs", 0, 1), ("ag", 3, 1), ("rs", 2, 0), ("rs", 1, 1), ("weights_on", 3), ("ag", 4, 1), ("grad_part", 2),
-    ("rs", 0, 2), ("rs", 3, 0), ("rs", 2, 1), ("grad_part", 3), ("rs", 0, 3), ("rotated", 1), ("weight_grad", 1),
-    ("rs", 1, 2), ("rs_end", 0), ("rs", 3, 1), ("ag", 2, 3), ("rs", 1, 3), ("had3", 1, 0), ("rs", 2, 2),
-    ("rs_end", 1), ("last_part", 0), ("ag", 3, 2), ("rs", 2, 3), ("had3", 1, 1), ("rs", 3, 2), ("ag", 3, 3),
-    ("last_part", 1), ("ag", 3, 0), ("rs", 3, 3), ("rs_end", 2), ("ag", 4, 2), ("ag", 4, 3), ("ag", 4, 0),
-    ("had3", 1, 2), ("rs_end", 3), ("rotated", 2), ("weight_grad", 2), ("rotated", 3), ("weight_grad", 3),
-    ("rotated", 0), ("weight_grad", 0), ("ls_send",), ("had3", 1, 3), ("last_part", 2), ("ls_end",), ("last_part", 3),
+    ("hidden",), ("mixed", 0), ("weights", 0), ("mixed", 1), ("had3", 0, 0), ("mixed", 2), ("weights", 1),
+    ("had3", 0, 1), ("mixed", 3), ("ag", 1, 0), ("weights_on", 0), ("had3", 0, 2), ("ag", 1, 1), ("og_on",),
+    ("weights", 2), ("ag", 2, 0), ("had3", 0, 3), ("weights", 3), ("ag", 1, 2), ("grad_part", 0), ("rs", 0, 0),
+    ("ag", 3, 0), ("ag", 2, 2), ("rs", 1, 0), ("ag", 2, 1), ("ag", 1, 3), ("weights_on", 1), ("weights_on", 3),
+    ("rs", 2, 0), ("grad_part", 1), ("rs", 0, 1), ("ag", 3, 1), ("weights_on", 2), ("grad_part", 3), ("rs", 0, 3),
+    ("rs", 1, 1), ("grad_part", 2), ("rs", 0, 2), ("rs", 1, 3), ("rs", 2, 1), ("rs", 1, 2), ("ag", 4, 1),
+    ("rs", 3, 0), ("rs", 2, 3), ("ag", 4, 0), ("rs", 2, 2), ("rs", 3, 1), ("rs_end", 0), ("ag", 2, 3), ("rs", 3, 3),
+    ("ag", 3, 2), ("rotated", 1), ("rotated", 0), ("rs_end", 1), ("rs", 3, 2), ("had3", 1, 0), ("ag", 3, 3),
+    ("weight_grad", 0), ("weight_grad", 1), ("rs_end", 3), ("rs_end", 2), ("ag", 4, 2), ("had3", 1, 1), ("ag", 4, 3),
+    ("last_part", 0), ("had3", 1, 3), ("rotated", 2), ("weight_grad", 2), ("had3", 1, 2), ("rotated", 3),
+    ("weight_grad", 3), ("ls_send",), ("last_part", 1), ("last_part", 3), ("last_part", 2), ("ls_end",),
 )
 
 def rows_of(n):

time: 100 us -> 97.5 us (0.975)
  Pallas kernels: 98.6 us -> 96.8 us
    pallas_call x1, Pallas kernels: 96.2 us -> 94.3 us  [on_device(): pl.pallas_call(kernel, out_shape=(jax.ShapeDtypeStruct((BLK, TOK), F32),...]
where the time goes in v4:
time: 97.5 us; the launch traced here: 97.4 us
  Pallas kernels  96.8 us (99%)
    pallas_call x1, Pallas kernels, on_device(): pl.pallas_call(kernel, out_shape=(jax.ShapeDtypeStruct((BLK, TOK), F32),...  94.3 us
    pallas_call x1, Pallas kernels, on_device(): pl.pallas_call(finish, grid=(2,), out_shape=(jax.ShapeDtypeStruct((BLK, T...  2.41 us

profile of v4, /device:TPU:8, one launch (start us, length us, event | category | flops | bytes accessed | tf_op | source)
XLA Modules:
  0.0 97.4 jit_solution(15976358881287309169)
XLA Ops:
  0.6 94.3 %whole.1 = (f32[1600,128]{1,0:T(8,128)}, f32[32,320]{1,0:T(8,128)}) custom-call(bf16[128,5120]{1,0:T(8,128)(2,1)} %og_in.1, bf16[1600,128]{1,0:T(8,128)(2,1)} %bitcast.7, bf16[1600,128]{1,0:T(8,128)(2,1)} %bitcast.9, s32[320,1600]{1,0:T(8,128)} %codes_in.1, s32[25,320]{1,0:T(8,128)} %bitcast.11, f32[25,320]{1,0:T(8,128)} %bitcast.12, bf16[1600,1600]{1,0:T(8,128)(2,1)} %rot_in.1), custom_call_target="tpu_custom_call" | custom-call | tf_op jit(solution)/shard_map/whole/pallas_call | solution.py:417
  95.0 2.4 %finish.1 = (bf16[1600,128]{1,0:T(8,128)(2,1)}, bf16[1600,128]{1,0:T(8,128)(2,1)}, f32[25,320]{1,0:T(8,128)}) custom-call(f32[1600,128]{1,0:T(8,128)} %get-tuple-element.8.gh, bf16[1600,128]{1,0:T(8,128)(2,1)} %bitcast.8, bf16[1600,128]{1,0:T(8,128)(2,1)} %bitcast.10, f32[32,320]{1,0:T(8,128)} %get-tuple-element.9.ls), custom_call_target="tpu_custom_call" | custom-call | tf_op jit(solution)/shard_map/finish/pallas_call | solution.py:464
